TPU v7x, 128 devices: a whole 4x4x4 slice. The times are simulated.
128 devices in a mesh: pool: 4 (over y), seq: 32 (over x, z, core).
Axes of the slice: x: 4, y: 4, z: 4, core: 2. Of those that a mesh axis runs over, the one named last changes fastest.
Arguments:
- pool_kv: bfloat16 [16, 4096, 1024], P('pool', 'seq'), may hold values from -4 to 4
- span_home: int32 [12], replicated, may hold values from 0 to 15, as said below
- span_order: int32 [4, 3], P('pool'), may hold values from 0 to 11, as said below
- chosen: int32 [4, 14], P('pool'), may hold values from 0 to 95, as said below
- fresh_q: bfloat16 [4, 1792, 6144], P('pool', 'seq'), may hold values from -300 to 300
- fresh_kv: bfloat16 [4, 1792, 1024], P('pool', 'seq'), may hold values from -5 to 5
Outputs:
- attended: bfloat16 [4, 1792, 6144], P('pool', 'seq')
- decode_kv: bfloat16 [4, 32, 4, 96, 1024], P('pool', 'seq')
Inputs may be any that keep to these rules, and one draw needn't show every extreme that they name: `span_home`: all entries differ; home // 4 is the replica of a passage, and the 3 passages r * 3 to r * 3 + 2 of request r lie on different replicas; some replica holds a passage of every request. `span_order`: row r orders the passages r * 3 to r * 3 + 2. `chosen`: each row lists 14 different blocks in rising order; block k holds positions k * 128 to k * 128 + 127.
All inputs are finite; a program needn't handle non-finite values.
Results may differ from a plain program's by a relative error of at most 0.0035.
Values may be sent and summed in bfloat16 or wider, within the bound.
A program may use at most 192 MiB of HBM per device.

v0:
```python
import math

import jax
import jax.numpy as jnp
from jax import lax
from jax.sharding import PartitionSpec as P

KV_HEADS = 4
HEAD_DIM = 128


masked_low = -1e30


def patch_rows(values, positions, picked, fresh_all, block_len):
    block_ids = positions // block_len
    offsets = positions % block_len
    matches = block_ids[..., None] == picked
    is_fresh = jnp.any(matches, axis=-1)
    slot_ids = jnp.sum(jnp.where(matches, jnp.arange(picked.shape[0], dtype=jnp.int32), 0), axis=-1)
    source = (slot_ids * block_len + offsets).reshape(-1)
    rows_new = jnp.take(fresh_all, source, axis=0).reshape(values.shape)
    return jnp.where(is_fresh[..., None], rows_new, values)


def fold_keys(state_in, shard_piece, queries, query_pos, span_len):
    span_count, piece_rows, kv_width = shard_piece.shape
    key_pos = (
        jnp.arange(span_count, dtype=jnp.int32)[:, None] * span_len
        + jnp.arange(piece_rows, dtype=jnp.int32)[None, :]
    )
    kv_heads, query_rows, head_dim = queries.shape
    flattened = shard_piece.reshape(span_count * piece_rows, kv_heads, 2, head_dim)
    keys_all = flattened[:, :, 0]
    values_all = flattened[:, :, 1]
    pos_all = key_pos.reshape(-1)
    key_count = span_count * piece_rows
    step_len = math.gcd(key_count, 512)
    inv_root = head_dim ** (-0.5)

    def one_block(state_now, turn_at):
        running_max, total_weight, weighted = state_now
        first_key = turn_at * step_len
        key_blk = lax.dynamic_slice_in_dim(keys_all, first_key, step_len, 0)
        value_blk = lax.dynamic_slice_in_dim(values_all, first_key, step_len, 0)
        pos_blk = lax.dynamic_slice_in_dim(pos_all, first_key, step_len, 0)
        scores = (
            jnp.einsum("hqd,khd->hqk", queries, key_blk, preferred_element_type=jnp.float32)
            * inv_root
        )
        allowed = pos_blk[None, None, :] <= query_pos[None, :, None]
        scores = jnp.where(allowed, scores, masked_low)
        newest = jnp.maximum(running_max, jnp.max(scores, axis=-1))
        weights = jnp.where(allowed, jnp.exp(scores - newest[..., None]), 0.0)
        factor = jnp.exp(running_max - newest)
        total_weight = total_weight * factor + jnp.sum(weights, axis=-1)
        weighted = weighted * factor[..., None] + jnp.einsum(
            "hqk,khd->hqd",
            weights.astype(jnp.bfloat16),
            value_blk,
            preferred_element_type=jnp.float32,
        )
        return ((newest, total_weight, weighted), None)

    state_out, _ = lax.scan(one_block, state_in, jnp.arange(key_count // step_len))
    return state_out


def shards(pool_kv, span_home, span_order, chosen, fresh_q, fresh_kv):
    pool_count = lax.axis_size("pool")
    seq_count = lax.axis_size("seq")
    replica = lax.axis_index("pool")
    my_seat = lax.axis_index("seq")
    slot_count, block_len, kv_width = pool_kv.shape
    span_count = span_order.shape[1]
    span_len = block_len * seq_count
    head_dim = HEAD_DIM
    kv_heads = KV_HEADS
    picked = chosen[0]
    span_total = span_home.shape[0]
    home_replica = span_home // slot_count
    home_slot = span_home % slot_count
    span_request = jnp.arange(span_total, dtype=jnp.int32) // span_count
    requests = jnp.arange(pool_count, dtype=jnp.int32)
    held = (home_replica == replica)[None, :] & (span_request[None, :] == requests[:, None])
    in_slot = home_slot[None, :, None] == jnp.arange(slot_count, dtype=jnp.int32)[None, None, :]
    selector = jnp.any(held[:, :, None] & in_slot, axis=1).astype(jnp.bfloat16)
    outgoing = jnp.einsum(
        "rk,ktc->rtc", selector, pool_kv, preferred_element_type=jnp.float32
    ).astype(jnp.bfloat16)
    arrived = lax.all_to_all(outgoing, "pool", split_axis=0, concat_axis=0, tiled=True)
    order_row = span_order[0]
    lookup = order_row[:, None] == jnp.arange(span_total, dtype=jnp.int32)[None, :]
    source_replica = jnp.sum(jnp.where(lookup, home_replica[None, :], 0), axis=1)
    chooser = (source_replica[:, None] == requests[None, :]).astype(jnp.bfloat16)
    cached = jnp.einsum("jp,ptc->jtc", chooser, arrived, preferred_element_type=jnp.float32).astype(
        jnp.bfloat16
    )
    fresh_all = lax.all_gather(fresh_kv[0], "seq", axis=0, tiled=True)
    block_ids = jnp.arange(span_count, dtype=jnp.int32)[:, None] * seq_count + my_seat
    local_pos = block_ids * block_len + jnp.arange(block_len, dtype=jnp.int32)[None, :]
    patched = patch_rows(cached, local_pos, picked, fresh_all, block_len)
    row_count = fresh_q.shape[1]
    q_width = fresh_q.shape[2]
    group = q_width // (kv_heads * head_dim)
    list_rows = my_seat * row_count + jnp.arange(row_count, dtype=jnp.int32)
    list_block = list_rows // block_len
    base_block = jnp.sum(
        jnp.where(
            list_block[:, None] == jnp.arange(picked.shape[0], dtype=jnp.int32)[None, :],
            picked[None, :],
            0,
        ),
        axis=1,
    )
    query_pos = base_block * block_len + list_rows % block_len
    queries = fresh_q[0].reshape(row_count, kv_heads, group, head_dim).transpose(1, 2, 0, 3)
    queries = queries.reshape(kv_heads, group * row_count, head_dim)
    pos_tiled = jnp.tile(query_pos, group)
    start_state = (
        jnp.full((kv_heads, group * row_count), masked_low, jnp.float32),
        jnp.zeros((kv_heads, group * row_count), jnp.float32),
        jnp.zeros((kv_heads, group * row_count, head_dim), jnp.float32),
    )
    final_state = fold_keys(
        start_state,
        lax.all_gather(patched, "seq", axis=1, tiled=True),
        queries,
        pos_tiled,
        span_len,
    )
    running_max, total_weight, weighted = final_state
    attended = (weighted / total_weight[..., None]).reshape(kv_heads, group, row_count, head_dim)
    attended = attended.transpose(2, 0, 1, 3).reshape(1, row_count, q_width).astype(jnp.bfloat16)
    per_group = kv_heads // pool_count
    run_len = block_len // seq_count
    laid = patched.reshape(span_count, seq_count, run_len, pool_count, per_group, 2 * head_dim)
    laid = laid.transpose(3, 1, 4, 0, 2, 5).reshape(
        pool_count, seq_count, per_group, span_count, run_len * 2 * head_dim
    )
    merged = laid.reshape(pool_count * seq_count, per_group, span_count, run_len * 2 * head_dim)
    landed = lax.all_to_all(merged, ("pool", "seq"), split_axis=0, concat_axis=0, tiled=True)
    landed = landed.reshape(pool_count, seq_count, per_group, span_count, run_len * 2 * head_dim)
    decoded = landed.transpose(2, 0, 3, 1, 4).reshape(
        per_group, 1, pool_count, span_count * seq_count, run_len * 2 * head_dim
    )
    return (attended, decoded)


def solution(mesh):
    in_specs = (
        P("pool", "seq", None),
        P(),
        P("pool", None),
        P("pool", None),
        P("pool", "seq", None),
        P("pool", "seq", None),
    )
    out_specs = (P("pool", "seq", None), P("pool", "seq", None, None, None))
    return jax.shard_map(shards, mesh=mesh, in_specs=in_specs, out_specs=out_specs, check_vma=False)
```

profile of v0, /device:TPU:1, one launch (start us, length us, event | category | flops | bytes accessed | tf_op | source)
XLA Modules:
  0.0 632.1 jit_solution(8040437564425881074)
XLA Ops:
  11.7 5.0 all-to-all-start
  17.5 42.0 %all-gather.6.cloned.1.call-done = bf16[1,1792,1024]{2,1,0:T(8,128)(2,1)} async-done(((bf16[1,56,1024]{2,1,0:T(8,128)(2,1)}), bf16[1,1792,1024]{2,1,0:T(8,128)(2,1)}) %all-gather.6.cloned.1.call-update) | async-done | bytes 3670032 | tf_op jit(solution)/shard_map/all_gather | solution.py:99
  59.5 5.3 gather_fusion
  71.5 7.2 %all-to-all-start.1 = ((bf16[128,1,3,1024]{3,2,1,0:T(4,128)(2,1)}), bf16[128,1,3,1024]{3,2,1,0:T(4,128)(2,1)S(1)}, u32[]{:S(2)}, u32[]{:S(2)}) async-start(bf16[128,1,3,1024]{3,2,1,0:T(4,128)(2,1)} %reshape.349), calls=%async_computation.1 | async-start | bytes 2097152 | tf_op jit(solution)/shard_map/all_to_all | solution.py:142
  81.1 27.9 %all-to-all-done.1 = bf16[128,1,3,1024]{3,2,1,0:T(4,128)(2,1)S(1)} async-done(((bf16[128,1,3,1024]{3,2,1,0:T(4,128)(2,1)}), bf16[128,1,3,1024]{3,2,1,0:T(4,128)(2,1)S(1)}, u32[]{:S(2)}, u32[]{:S(2)}) %all-to-all-start.1) | async-done | bytes 786464 | tf_op jit(solution)/shard_map/all_to_all | solution.py:142
  110.2 60.9 %all-gather.4.cloned.1.call-done = bf16[3,4096,1024]{2,1,0:T(8,128)(2,1)} async-done(((bf16[3,128,1024]{2,1,0:T(8,128)(2,1)}), bf16[3,4096,1024]{2,1,0:T(8,128)(2,1)}) %all-gather.4.cloned.1.call-update) | async-done | bytes 25165840 | tf_op jit(solution)/shard_map/all_gather | solution.py:127
  171.1 40.5 %reshape.332 = bf16[12288,4,2,128]{3,2,1,0:T(2,128)(2,1)} reshape(bf16[3,4096,1024]{2,1,0:T(8,128)(2,1)} %all-gather.4.cloned.1.call-done) | data formatting | bytes 50331648 | tf_op jit(solution)/shard_map/reshape | solution.py:33
  211.6 47.1 %fusion.38 = (bf16[12288,4,1,128]{3,2,1,0:T(2,128)(2,1)}, bf16[12288,4,1,128]{3,2,1,0:T(2,128)(2,1)}) fusion(bf16[12288,4,2,128]{3,2,1,0:T(2,128)(2,1)} %reshape.332), kind=kLoop, calls=%fused_computation.93 | loop fusion | bytes 50331648 | tf_op jit(solution)/shard_map/slice | solution.py:35
  258.7 27.3 %copy_bitcast_fusion = (bf16[12288,4,128]{2,0,1:T(8,128)(2,1)}, bf16[12288,4,128]{2,0,1:T(8,128)(2,1)}) fusion(bf16[12288,4,1,128]{3,2,1,0:T(2,128)(2,1)} %get-tuple-element.129, bf16[12288,4,1,128]{3,2,1,0:T(2,128)(2,1)} %get-tuple-element.130), kind=kLoop, calls=%fused_computation.24 | loop fusion | bytes 50331648 | tf_op jit(solution)/shard_map/squeeze | solution.py:35
  286.1 337.2 %while.15 = (s32[]{:T(128)}, f32[4,672]{1,0:T(4,128)S(1)}, f32[4,672]{1,0:T(4,128)S(1)}, f32[4,672,128]{2,1,0:T(8,128)S(1)}, s32[24]{0:T(128)S(1)}, /*index=5*/s...) while((s32[]{:T(128)}, f32[4,672]{1,0:T(4,128)S(1)}, ...), condition=%wide.region_8.9_spmd.clone, body=%wide.region_5.8_spmd.clone.sunk | while | flops 723924096 | bytes 44590032 | solution.py:65
  287.9 4.5 fusion.50
  292.4 4.4 fusion.51
  301.9 4.5 fusion.50
  306.4 4.4 fusion.51
  316.0 4.5 fusion.50
  320.5 4.4 fusion.51
  330.0 4.5 fusion.50
  334.5 4.4 fusion.51
  344.1 4.5 fusion.50
  348.6 4.4 fusion.51
  358.1 4.5 fusion.50
  372.2 4.5 fusion.50
  386.2 4.5 fusion.50
  390.7 4.4 fusion.51
  400.3 4.5 fusion.50
  404.8 4.4 fusion.51
  414.3 4.5 fusion.50
  418.8 4.4 fusion.51
  428.4 4.5 fusion.50
  442.4 4.5 fusion.50
  446.9 4.4 fusion.51
  456.5 4.5 fusion.50
  461.0 4.4 fusion.51
  470.5 4.5 fusion.50
  475.0 4.4 fusion.51
  484.6 4.5 fusion.50
  489.1 4.4 fusion.51
  498.6 4.5 fusion.50
  503.1 4.4 fusion.51
  512.7 4.5 fusion.50
  526.7 4.5 fusion.50
  531.2 4.4 fusion.51
  540.8 4.5 fusion.50
  554.8 4.5 fusion.50
  568.9 4.5 fusion.50
  582.9 4.5 fusion.50
  597.0 4.5 fusion.50
  611.0 4.5 fusion.50
  (331 shorter events, 167.1 us)
Async XLA Ops:
  7.2 2.3 copy-start
  7.2 9.6 %copy-start.4 = (s32[1,14]{1,0:T(1,128)S(1)}, s32[1,14]{1,0:T(1,128)}, u32[]{:S(2)}) copy-start(s32[1,14]{1,0:T(1,128)} %param.11) | copy-start | bytes 172
  7.2 10.2 %copy-start.5 = (s32[1,3]{1,0:T(1,128)S(1)}, s32[1,3]{1,0:T(1,128)}, u32[]{:S(2)}) copy-start(s32[1,3]{1,0:T(1,128)} %param.10) | copy-start | bytes 40
  7.2 52.3 %all-gather.6.cloned.1.call-start = ((), (), s32[]{:S(2)}) async-start(), calls=%async_computation.3 | async-start | bytes 3784704 | tf_op jit(solution)/shard_map/all_gather | solution.py:99
  11.7 53.2 %all-to-all-start = ((bf16[4,128,1024]{2,1,0:T(8,128)(2,1)}), bf16[4,128,1024]{2,1,0:T(8,128)(2,1)S(1)}, u32[]{:S(2)}, u32[]{:S(2)}) async-start(bf16[4,128,1024]{2,1,0:T(8,128)(2,1)} %copy.49), calls=%async_computation | async-start | bytes 2097152 | tf_op jit(solution)/shard_map/all_to_all | solution.py:91
  16.6 154.5 %all-gather.4.cloned.1.call-start = ((), (), s32[]{:S(2)}) async-start(), calls=%async_computation.2 | async-start | bytes 25952256 | tf_op jit(solution)/shard_map/all_gather | solution.py:127
  71.5 37.4 %all-to-all-start.1 = ((bf16[128,1,3,1024]{3,2,1,0:T(4,128)(2,1)}), bf16[128,1,3,1024]{3,2,1,0:T(4,128)(2,1)S(1)}, u32[]{:S(2)}, u32[]{:S(2)}) async-start(bf16[128,1,3,1024]{3,2,1,0:T(4,128)(2,1)} %reshape.349), calls=%async_computation.1 | async-start | bytes 2097152 | tf_op jit(solution)/shard_map/all_to_all | solution.py:142
  258.7 27.3 %copy-start.3 = (f32[4,672,128]{2,1,0:T(8,128)S(1)}, f32[4,672,128]{2,1,0:T(8,128)}, u32[]{:S(2)}) copy-start(f32[4,672,128]{2,1,0:T(8,128)} %custom-call.2) | copy-start | bytes 4128772
  292.4 4.4 copy-start.2
  306.4 4.4 copy-start.2
  320.5 4.4 copy-start.2
  334.5 4.4 copy-start.2
  348.6 4.4 copy-start.2
  362.6 4.4 copy-start.2
  376.7 4.4 copy-start.2
  390.7 4.4 copy-start.2
  404.8 4.4 copy-start.2
  418.8 4.4 copy-start.2
  432.9 4.4 copy-start.2
  446.9 4.4 copy-start.2
  461.0 4.4 copy-start.2
  475.0 4.4 copy-start.2
  489.1 4.4 copy-start.2
  503.1 4.4 copy-start.2
  517.2 4.4 copy-start.2
  531.2 4.4 copy-start.2
  545.3 4.4 copy-start.2
  559.3 4.4 copy-start.2
  573.4 4.4 copy-start.2
  587.4 4.4 copy-start.2
  601.5 4.4 copy-start.2
  615.5 4.4 copy-start.2
  623.3 2.0 copy-start.1
Sparse Core Ops, SparseCore 0:
  10.3 49.2 all-gather.5
  69.1 102.0 all-gather.3
where the time goes:
time: 636 us; the launch traced here: 632 us
  matrix products  191 us (30%)
  local copies, waits for them, and re-layouts  150 us (24%)
  waiting for transfers between devices  131 us (21%)
  other arithmetic  114 us (18%)
  loops' own time  18.3 us (3%)
  between operations  14.3 us (2%)
  starting transfers between devices  12.2 us (2%)
    dot_general x24, matrix products, one_block(): jnp.einsum('hqd,khd->hqk', queries, key_blk, preferred_element_type=jnp.f...  108 us
    reduce_sum x24, other arithmetic, one_block(): total_weight = total_weight * factor + jnp.sum(weights, axis=-1)  105 us
    dot_general x24, matrix products, one_block(): jnp.einsum('hqk,khd->hqd', weights.astype(jnp.bfloat16), value_blk, prefe...  79.2 us
    all_gather x1, waiting for transfers between devices, shards(): lax.all_gather(patched, 'seq', axis=1, tiled=True)  60.9 us
    slice x1, local copies, waits for them, and re-layouts, fold_keys(): values_all = flattened[:, :, 1]  47.1 us
    all_gather x1, waiting for transfers between devices, shards(): fresh_all = lax.all_gather(fresh_kv[0], 'seq', axis=0, tiled=True)  42 us
    reshape x1, local copies, waits for them, and re-layouts, fold_keys(): shard_piece.reshape(span_count * piece_rows, kv_heads, 2, head_dim)  40.5 us
    all_to_all x1, waiting for transfers between devices, shards(): lax.all_to_all(merged, ('pool', 'seq'), split_axis=0, concat_axis=0, tile...  27.9 us
  transfers between devices with their start and end apart: 4, of which 3 were waited for; matrix products, arithmetic and copies ran while one was open for 3% of the time, Pallas kernels for 0%

commit v1 on v0

v1 whole, which is shorter than its diff:
```python
import functools
import math

import jax
import jax.numpy as jnp
from jax import lax
from jax.experimental import pallas as pl
from jax.experimental.pallas import tpu as pltpu
from jax.sharding import PartitionSpec as P

MESH = pl.DeviceIdType.MESH
ANY = pl.BlockSpec(memory_space=pl.ANY)
IN_VMEM = pl.BlockSpec(memory_space=pltpu.VMEM)

POOL = 4
HEADS = 4
GROUP = 12
DIM = 128
BLOCK = 128
SPANS = 3
ROWS = 56
PICKED = 14
BLOCKS = 96
WIDE = GROUP * DIM
PAIR = 2 * DIM
CHUNK = 8
STEPS = BLOCKS // CHUNK
KEYS = CHUNK * BLOCK
TILE = 16 * GROUP
LOW = -1e30


def seat(x, z, c):
    return (x * 4 + z) * 2 + c


def here():
    y = lax.axis_index("pool")
    s = lax.axis_index("seq")
    return y, s, s // 8, (s // 2) % 4, s % 2


def remote(src, dst, send, recv, y, s):
    return pltpu.make_async_remote_copy(
        src_ref=src, dst_ref=dst, send_sem=send, recv_sem=recv, device_id=(y, s), device_id_type=MESH
    )


def greet_plane(barrier, y, s):
    def one(d, carry):
        pl.semaphore_signal(barrier, inc=1, device_id=(y, (s + d) % 32), device_id_type=MESH)
        return carry

    lax.fori_loop(1, 32, one, 0)


def pick_kernel(index, src, dst):
    dst[...] = src[...]


def pick_blocks(stack, index, count):
    rows, cols = stack.shape[1:]
    return pl.pallas_call(
        pick_kernel,
        out_shape=jax.ShapeDtypeStruct((count, rows, cols), stack.dtype),
        grid_spec=pltpu.PrefetchScalarGridSpec(
            num_scalar_prefetch=1,
            grid=(count,),
            in_specs=[pl.BlockSpec((1, rows, cols), lambda i, index: (index[i], 0, 0))],
            out_specs=pl.BlockSpec((1, rows, cols), lambda i, index: (i, 0, 0)),
        ),
    )(index, stack)


def first_kernel(out_ref, q_ref, f_ref, arr_ref, qx_ref, fz_ref, hold, y_send, y_recv, q_send, q_recv, f_send, f_recv, l_sem):
    y, s, x, z, c = here()
    barrier = pltpu.get_barrier_semaphore()
    greet_plane(barrier, y, s)
    for d in range(1, POOL):
        pl.semaphore_signal(barrier, inc=1, device_id=((y + d) % POOL, s), device_id_type=MESH)
    own_in = pltpu.make_async_copy(out_ref.at[y], hold, l_sem.at[0])
    own_in.start()
    pl.semaphore_wait(barrier, 31 + POOL - 1)

    passages = []
    for d in (2, 1, 3):
        to = (y + d) % POOL
        copy = remote(out_ref.at[to], arr_ref.at[y], y_send.at[d - 1], y_recv.at[d - 1], to, s)
        copy.start()
        passages.append(copy)
    fresh = []
    for d in (1, 2, 3):
        to = (z + d) % 4
        copy = remote(
            f_ref.at[:, pl.ds(pl.multiple_of(to * PAIR, PAIR), PAIR)],
            fz_ref.at[z],
            f_send.at[d - 1],
            f_recv.at[d - 1],
            y,
            seat(x, to, c),
        )
        copy.start()
        fresh.append(copy)
    own_fresh = pltpu.make_async_copy(
        f_ref.at[:, pl.ds(pl.multiple_of(z * PAIR, PAIR), PAIR)], fz_ref.at[z], l_sem.at[1]
    )
    own_fresh.start()

    def piece(t):
        k, h = t // 4, t % 4
        m = 7 * s + k
        g = m % 8
        to = seat(g // 2, h, g % 2)
        src = q_ref.at[pl.ds(pl.multiple_of(k * 8, 8), 8), pl.ds(pl.multiple_of(h * WIDE, WIDE), WIDE)]
        dst = qx_ref.at[pl.ds(pl.multiple_of((m // 8) * 8, 8), 8), :]
        return src, dst, to

    def send(t, carry):
        src, dst, to = piece(t)

        @pl.when(to != s)
        def _():
            remote(src, dst, q_send.at[t], q_recv, y, to).start()

        @pl.when(to == s)
        def _():
            pltpu.make_async_copy(src, dst, q_recv).start()

        return carry

    lax.fori_loop(0, 28, send, 0)
    own_in.wait()
    own_out = pltpu.make_async_copy(hold, arr_ref.at[y], l_sem.at[0])
    own_out.start()

    def sent(t, carry):
        src, dst, to = piece(t)

        @pl.when(to != s)
        def _():
            remote(src, dst, q_send.at[t], q_recv, y, to).wait_send()

        return carry

    lax.fori_loop(0, 28, sent, 0)
    remote(qx_ref, qx_ref, q_send.at[0], q_recv, y, (s + 1) % 32).wait_recv()
    own_fresh.wait()
    own_out.wait()
    for copy in fresh:
        copy.wait()
    for copy in passages:
        copy.wait()


def first_exchange(outgoing, fresh_q, fresh_kv):
    bf16 = jnp.bfloat16
    dma = pltpu.SemaphoreType.DMA
    return pl.pallas_call(
        first_kernel,
        out_shape=(
            jax.ShapeDtypeStruct((POOL, BLOCK, 1024), bf16),
            jax.ShapeDtypeStruct((4 * ROWS, WIDE), bf16),
            jax.ShapeDtypeStruct((4, ROWS, PAIR), bf16),
        ),
        in_specs=[ANY] * 3,
        out_specs=(ANY,) * 3,
        scratch_shapes=[
            pltpu.VMEM((BLOCK, 1024), bf16),
            dma((3,)),
            dma((3,)),
            dma((28,)),
            dma,
            dma((3,)),
            dma((3,)),
            dma((2,)),
        ],
        compiler_params=pltpu.CompilerParams(collective_id=0, has_side_effects=True),
        name="first_exchange",
    )(outgoing, fresh_q, fresh_kv)


def gather_kernel(kv_ref, fz_ref, all_ref, fr_ref, z_send, z_recv, x_send, x_recv, h_send, h_recv, c_send, c_recv, l_sem):
    y, s, x, z, c = here()
    right, left = (x + 1) % 4, (x + 3) % 4
    far = (x + 2) % 4
    across = seat(x, z, 1 - c)
    barrier = pltpu.get_barrier_semaphore()
    for d in (1, 2, 3):
        pl.semaphore_signal(barrier, inc=1, device_id=(y, seat(x, (z + d) % 4, c)), device_id_type=MESH)
    for to in (seat(right, z, c), seat(left, z, c), across):
        pl.semaphore_signal(barrier, inc=1, device_id=(y, to), device_id_type=MESH)
    pl.semaphore_wait(barrier, 6)

    def head(h):
        return kv_ref.at[:, :, pl.ds(pl.multiple_of(h * PAIR, PAIR), PAIR)]

    shifts = (0, 1, 3, 2)
    pending = []
    z_in = {}
    for d in (1, 3, 2):
        to = (z + d) % 4
        copy = remote(head(to), all_ref.at[x, z, c], z_send.at[d - 1], z_recv.at[d - 1], y, seat(x, to, c))
        copy.start()
        z_in[4 - d] = copy
        pending.append(copy)
    own = pltpu.make_async_copy(head(z), all_ref.at[x, z, c], l_sem.at[0])
    own.start()
    own_fresh = pltpu.make_async_copy(fz_ref, fr_ref.at[x, :, c], l_sem.at[1])
    own_fresh.start()

    def view(p, at, core):
        if p == 0:
            return fr_ref.at[at, :, core]
        return all_ref.at[at, (z + shifts[p - 1]) % 4, core]

    def half(p, at, core, side):
        if p == 0:
            return fr_ref.at[at, pl.ds(2 * side, 2), core]
        return all_ref.at[at, (z + shifts[p - 1]) % 4, core, :, pl.ds(64 * side, 64)]

    def ring(p, way):
        to = right if way == 0 else left
        return remote(view(p, x, c), view(p, x, c), x_send.at[way, p], x_recv.at[way, p], y, seat(to, z, c))

    def ring_in(p, way):
        at = left if way == 0 else right
        return remote(view(p, at, c), view(p, at, c), x_send.at[way, p], x_recv.at[way, p], y, seat(at, z, c))

    def onward(p, way):
        at, to = (left, right) if way == 0 else (right, left)
        return remote(half(p, at, c, way), half(p, at, c, way), h_send.at[way, p], h_recv.at[way, p], y, seat(to, z, c))

    def onward_in(p, way):
        return remote(half(p, far, c, way), half(p, far, c, way), h_send.at[way, p], h_recv.at[way, p], y, seat(left, z, c))

    def give(p, kind, core):
        if kind < 3:
            v = view(p, (x, left, right)[kind], core)
        else:
            v = half(p, far, core, kind - 3)
        return remote(v, v, c_send.at[kind, p], c_recv.at[kind, p], y, across)

    def start(copy):
        copy.start()
        pending.append(copy)

    def own_ready(p):
        if p == 0:
            own_fresh.wait()
        elif p == 1:
            own.wait()
        else:
            z_in[shifts[p - 1]].wait_recv()
        start(ring(p, 0))
        start(ring(p, 1))
        start(give(p, 0, c))

    def passed(p):
        for way in (0, 1):
            ring_in(p, way).wait_recv()
            start(onward(p, way))
            start(give(p, 1 + way, c))

    for p in range(5):
        own_ready(p)
    for p in range(5):
        passed(p)
    for p in range(5):
        for way in (0, 1):
            onward_in(p, way).wait_recv()
            start(give(p, 3 + way, c))
    for p in range(5):
        for kind in range(5):
            give(p, kind, 1 - c).wait_recv()
    for copy in pending:
        copy.wait_send()


def gather_head(cached, fz):
    bf16 = jnp.bfloat16
    dma = pltpu.SemaphoreType.DMA
    return pl.pallas_call(
        gather_kernel,
        out_shape=(
            jax.ShapeDtypeStruct((4, 4, 2, SPANS, BLOCK, PAIR), bf16),
            jax.ShapeDtypeStruct((4, 4, 2, ROWS, PAIR), bf16),
        ),
        in_specs=[IN_VMEM, IN_VMEM],
        out_specs=(ANY, ANY),
        scratch_shapes=[
            dma((3,)),
            dma((3,)),
            dma((2, 5)),
            dma((2, 5)),
            dma((2, 5)),
            dma((2, 5)),
            dma((5, 5)),
            dma((5, 5)),
            dma((2,)),
        ],
        compiler_params=pltpu.CompilerParams(collective_id=1, has_side_effects=True),
        name="gather_head",
    )(cached, fz)


def attend_kernel(chosen, group, kv_ref, fr_ref, qx_ref, att_ref, dec_ref, kv, fresh, q, top, acc, rows32, sems):
    g = group[0]
    bf16, f32 = jnp.bfloat16, jnp.float32

    def load(step):
        j, part = step // 4, step % 4
        return pltpu.make_async_copy(
            kv_ref.at[pl.ds(part * CHUNK, CHUNK), j], kv.at[pl.ds(step * CHUNK, CHUNK)], sems.at[step]
        )

    fresh_in = pltpu.make_async_copy(fr_ref, fresh, sems.at[STEPS])
    fresh_in.start()
    for step in range(STEPS):
        load(step).start()

    scale = math.log2(math.e) / math.sqrt(DIM)

    def prepare(i, carry):
        r0 = pl.multiple_of(i * 16, 16)
        for hd in range(GROUP):
            full = qx_ref[pl.ds(r0, 16), hd * DIM : (hd + 1) * DIM].astype(f32) * scale
            q[i, hd * 16 : (hd + 1) * 16, 0:DIM] = full.astype(bf16)
            high = q[i, hd * 16 : (hd + 1) * 16, 0:DIM].astype(f32)
            q[i, hd * 16 : (hd + 1) * 16, DIM:PAIR] = (full - high).astype(bf16)
        top[i] = jnp.full((TILE, DIM), LOW, f32)
        acc[i] = jnp.zeros((TILE, PAIR), f32)
        return carry

    lax.fori_loop(0, PICKED, prepare, 0)
    fresh_in.wait()

    def before(block):
        total = jnp.int32(0)
        for i in range(PICKED):
            total = total + jnp.where(chosen[i] < block, 1, 0).astype(jnp.int32)
        return total

    ones = jnp.ones((KEYS, DIM), bf16)

    def fold(i, n, keys, values, mask_from):
        qq = q[pl.ds(i, n)].reshape(n * TILE, PAIR)
        s = lax.dot_general(qq, keys, (((1,), (1,)), ((), ())), preferred_element_type=f32)
        if mask_from is not None:
            row = lax.broadcasted_iota(jnp.int32, (TILE, KEYS), 0)
            token = 64 * ((row % 16) // 8) + 8 * g + row % 8
            key = lax.broadcasted_iota(jnp.int32, (TILE, KEYS), 1)
            s = jnp.where(key <= token + mask_from, s, LOW)
        old = top[pl.ds(i, n)].reshape(n * TILE, DIM)
        new = jnp.maximum(old, jnp.max(s, axis=1, keepdims=True))
        w = jnp.exp2(s - new[:, 0:1]).astype(bf16)
        part = jnp.dot(w, values, preferred_element_type=f32)
        factor = jnp.exp2(old - new)
        both = jnp.concatenate([factor, factor], axis=1)
        acc[pl.ds(i, n)] = (acc[pl.ds(i, n)].reshape(n * TILE, PAIR) * both + part).reshape(n, TILE, PAIR)
        top[pl.ds(i, n)] = new.reshape(n, TILE, DIM)

    def step_body(step, first):
        load(step).wait()
        last = before((step + 1) * CHUNK)

        def patch(i, carry):
            kv[chosen[i]] = fresh[pl.ds(pl.multiple_of(i * BLOCK, BLOCK), BLOCK), :]
            return carry

        lax.fori_loop(first, last, patch, 0)

        at = step * CHUNK
        slab = kv[pl.ds(at, CHUNK), pl.ds(pl.multiple_of(g * 16, 16), 16), :].astype(f32)
        flat = slab.reshape(CHUNK * 16, PAIR)
        for side in range(2):
            rows32[side] = flat[:, side * DIM : (side + 1) * DIM]
        for k in range(4):
            for u in range(4):
                for side in range(2):
                    line = rows32[side, pl.ds(4 * k + u, CHUNK, stride=16), :]
                    to = u * PAIR + side * DIM
                    dec_ref[k, pl.ds(pl.multiple_of(at, CHUNK), CHUNK), to : to + DIM] = line.astype(bf16)

        both = kv[pl.ds(at, CHUNK)].reshape(KEYS, PAIR)
        keys = jnp.concatenate([both[:, :DIM], both[:, :DIM]], axis=1)
        values = jnp.concatenate([both[:, DIM:], ones], axis=1)

        def diagonal(i, carry):
            fold(i, 1, keys, values, (chosen[i] - at) * BLOCK)
            return carry

        lax.fori_loop(first, last, diagonal, 0)
        left = PICKED - last
        odd = left % 2

        @pl.when(odd == 1)
        def _():
            fold(last, 1, keys, values, None)

        def two(t, carry):
            fold(last + odd + 2 * t, 2, keys, values, None)
            return carry

        lax.fori_loop(0, left // 2, two, 0)
        return last

    lax.fori_loop(0, STEPS, step_body, jnp.int32(0))

    def finish(i, carry):
        out = acc[i, :, 0:DIM] / acc[i, :, DIM:PAIR]
        r0 = pl.multiple_of(i * 16, 16)
        for hd in range(GROUP):
            att_ref[pl.ds(r0, 16), hd * DIM : (hd + 1) * DIM] = out[hd * 16 : (hd + 1) * 16].astype(bf16)
        return carry

    lax.fori_loop(0, PICKED, finish, 0)


def attend(chosen, group, kv, fresh, qx):
    bf16, f32 = jnp.bfloat16, jnp.float32
    smem = pl.BlockSpec(memory_space=pltpu.SMEM)
    return pl.pallas_call(
        attend_kernel,
        out_shape=(
            jax.ShapeDtypeStruct((4 * ROWS, WIDE), bf16),
            jax.ShapeDtypeStruct((4, BLOCKS, 1024), bf16),
        ),
        in_specs=[smem, smem, ANY, ANY, IN_VMEM],
        out_specs=(IN_VMEM, IN_VMEM),
        scratch_shapes=[
            pltpu.VMEM((BLOCKS, BLOCK, PAIR), bf16),
            pltpu.VMEM((PICKED * BLOCK, PAIR), bf16),
            pltpu.VMEM((PICKED, TILE, PAIR), bf16),
            pltpu.VMEM((PICKED, TILE, DIM), f32),
            pltpu.VMEM((PICKED, TILE, PAIR), f32),
            pltpu.VMEM((2, CHUNK * 16, DIM), f32),
            pltpu.SemaphoreType.DMA((STEPS + 1,)),
        ],
        compiler_params=pltpu.CompilerParams(vmem_limit_bytes=48 * 1024 * 1024),
        name="attend",
    )(chosen, group, kv, fresh, qx)


def last_kernel(att_ref, dec_ref, out_ref, laid_ref, a_send, a_recv, d_send, d_recv):
    y, s, x, z, c = here()
    g = 2 * x + c
    barrier = pltpu.get_barrier_semaphore()
    greet_plane(barrier, y, s)
    giver = s // 4
    for d in range(1, POOL):
        source = seat(giver // 2, y, giver % 2)
        pl.semaphore_signal(barrier, inc=1, device_id=((y + d) % POOL, source), device_id_type=MESH)
    pl.semaphore_wait(barrier, 31 + jnp.where(z == y, 0, 4))

    def slab(k):
        return dec_ref.at[k], laid_ref.at[y], 4 * g + k

    def slab_send(k, carry):
        src, dst, to = slab(k)
        mine = jnp.logical_and(z == y, to == s)

        @pl.when(jnp.logical_not(mine))
        def _():
            remote(src, dst, d_send.at[k], d_recv, z, to).start()

        @pl.when(mine)
        def _():
            pltpu.make_async_copy(src, dst, d_recv).start()

        return carry

    lax.fori_loop(0, 4, slab_send, 0)

    def piece(j):
        m = 8 * j + g
        src = att_ref.at[pl.ds(pl.multiple_of(j * 8, 8), 8), :]
        dst = out_ref.at[
            pl.ds(pl.multiple_of((m % 7) * 8, 8), 8), pl.ds(pl.multiple_of(z * WIDE, WIDE), WIDE)
        ]
        return src, dst, m // 7

    def send(j, carry):
        src, dst, to = piece(j)

        @pl.when(to != s)
        def _():
            remote(src, dst, a_send.at[j], a_recv, y, to).start()

        @pl.when(to == s)
        def _():
            pltpu.make_async_copy(src, dst, a_recv).start()

        return carry

    lax.fori_loop(0, 28, send, 0)

    def slab_sent(k, carry):
        src, dst, to = slab(k)
        mine = jnp.logical_and(z == y, to == s)

        @pl.when(jnp.logical_not(mine))
        def _():
            remote(src, dst, d_send.at[k], d_recv, z, to).wait_send()

        return carry

    lax.fori_loop(0, 4, slab_sent, 0)

    def sent(j, carry):
        src, dst, to = piece(j)

        @pl.when(to != s)
        def _():
            remote(src, dst, a_send.at[j], a_recv, y, to).wait_send()

        return carry

    lax.fori_loop(0, 28, sent, 0)
    remote(out_ref, out_ref, a_send.at[0], a_recv, y, (s + 1) % 32).wait_recv()
    remote(laid_ref, laid_ref, d_send.at[0], d_recv, y, (s + 1) % 32).wait_recv()


def last_exchange(att, dec):
    bf16 = jnp.bfloat16
    dma = pltpu.SemaphoreType.DMA
    return pl.pallas_call(
        last_kernel,
        out_shape=(
            jax.ShapeDtypeStruct((ROWS, HEADS * WIDE), bf16),
            jax.ShapeDtypeStruct((POOL, BLOCKS, 1024), bf16),
        ),
        in_specs=[ANY, ANY],
        out_specs=(ANY, ANY),
        scratch_shapes=[dma((28,)), dma, dma((4,)), dma],
        compiler_params=pltpu.CompilerParams(collective_id=2, has_side_effects=True),
        name="last_exchange",
    )(att, dec)


def shards(pool_kv, span_home, span_order, chosen, fresh_q, fresh_kv):
    replica = lax.axis_index("pool")
    my_seat = lax.axis_index("seq")
    home_replica = span_home // 4
    home_slot = span_home % 4
    held = jnp.where(home_replica == replica, home_slot, 0).reshape(POOL, SPANS)
    outgoing = pick_blocks(pool_kv, jnp.sum(held, axis=1).astype(jnp.int32), POOL)
    arrived, qx, fz = first_exchange(outgoing, fresh_q[0], fresh_kv[0])
    lookup = span_order[0][:, None] == jnp.arange(POOL * SPANS, dtype=jnp.int32)[None, :]
    source = jnp.sum(jnp.where(lookup, home_replica[None, :], 0), axis=1).astype(jnp.int32)
    cached = pick_blocks(arrived, source, SPANS)
    kv, fresh = gather_head(cached, fz)
    group = (2 * (my_seat // 8) + my_seat % 2).astype(jnp.int32).reshape(1)
    att, dec = attend(
        chosen[0], group, kv.reshape(32, SPANS, BLOCK, PAIR), fresh.reshape(32 * ROWS, PAIR), qx
    )
    attended, laid = last_exchange(att, dec)
    return attended[None], laid[None, None]


def solution(mesh):
    in_specs = (
        P("pool", "seq", None),
        P(),
        P("pool", None),
        P("pool", None),
        P("pool", "seq", None),
        P("pool", "seq", None),
    )
    out_specs = (P("pool", "seq", None), P("pool", "seq", None, None, None))
    return jax.shard_map(shards, mesh=mesh, in_specs=in_specs, out_specs=out_specs, check_vma=False)
```

time: 636 us -> 203 us (0.32)
  Pallas kernels: 0 us -> 192 us
  matrix products: 191 us -> 0 us
  local copies, waits for them, and re-layouts: 150 us -> 8.13 us
  waiting for transfers between devices: 131 us -> 0 us
  other arithmetic: 114 us -> 2.66 us
  loops' own time: 18.3 us -> 0 us
  between operations: 14.3 us -> 0.72 us
  starting transfers between devices: 12.2 us -> 0 us
    pallas_call x0 -> x6, Pallas kernels: none -> 192 us  [the longest x1 78.8 us: attend(): pl.pallas_call(attend_kernel, out_shape=(jax.ShapeDtypeStruct((4 * ROWS,...]
    dot_general x50 -> x0, matrix products: 191 us -> none  [the longest x24 108 us: one_block(): jnp.einsum('hqd,khd->hqk', queries, key_blk, preferred_element_type=jnp.f...]
    reduce_sum x26 -> x1, other arithmetic: 105 us -> 0.63 us  [shards(): jnp.sum(held, axis=1).astype(jnp.int32)]
    all_gather x2 -> x0, waiting for transfers between devices: 103 us -> none  [the longest x1 60.9 us: shards(): lax.all_gather(patched, 'seq', axis=1, tiled=True)]
    slice x1 -> x0, local copies, waits for them, and re-layouts: 47.1 us -> none  [fold_keys(): values_all = flattened[:, :, 1]]
    reshape x3 -> x1, local copies, waits for them, and re-layouts: 41.5 us -> 0.08 us  [shards(): held = jnp.where(home_replica == replica, home_slot, 0).reshape(POOL, SPANS)]
    all_to_all x2 -> x0, waiting for transfers between devices: 27.9 us -> none  [the longest x1 27.9 us: shards(): lax.all_to_all(merged, ('pool', 'seq'), split_axis=0, concat_axis=0, tile...]
    squeeze x1 -> x0, local copies, waits for them, and re-layouts: 27.3 us -> none  [fold_keys(): values_all = flattened[:, :, 1]]
  transfers between devices with their start and end apart: 4 -> 0, of which waited for: 3 -> 0; matrix products, arithmetic and copies ran while one was open for 3% -> 0% of each run, Pallas kernels for 0% -> 0%
where the time goes in v1:
time: 203 us
  Pallas kernels  192 us (95%)
  local copies, waits for them, and re-layouts  8.13 us (4%)
  other arithmetic  2.66 us (1%)
    pallas_call x1, Pallas kernels, attend(): pl.pallas_call(attend_kernel, out_shape=(jax.ShapeDtypeStruct((4 * ROWS,...  78.8 us
    pallas_call x1, Pallas kernels, last_exchange(): pl.pallas_call(last_kernel, out_shape=(jax.ShapeDtypeStruct((ROWS, HEADS...  44.7 us
    pallas_call x1, Pallas kernels, gather_head(): pl.pallas_call(gather_kernel, out_shape=(jax.ShapeDtypeStruct((4, 4, 2, S...  37.7 us
    pallas_call x1, Pallas kernels, first_exchange(): pl.pallas_call(first_kernel, out_shape=(jax.ShapeDtypeStruct((POOL, BLOCK...  23.2 us
    unnamed x12, local copies, waits for them, and re-layouts  8.05 us
    pallas_call x2, Pallas kernels, pick_blocks(): pl.pallas_call(pick_kernel, out_shape=jax.ShapeDtypeStruct((count, rows,...  7.56 us

profile of v1, /device:TPU:1, one launch (start us, length us, event | category | flops | bytes accessed | tf_op | source)
XLA Modules:
  0.0 203.5 jit_solution(4217037926944916507)
XLA Ops:
  0.6 0.0 copy-start.4
  0.7 0.7 compare_select_fusion
  1.3 1.4 select_reduce_fusion.index
  2.7 0.1 reshape.19
  2.8 0.6 reduce_sum.19.index
  3.4 4.0 %shard_map.77.out_ref = bf16[4,128,1024]{2,1,0:T(8,128)(2,1)} custom-call(s32[4]{0:T(128)} %reduce_sum.19.index, bf16[4,128,1024]{2,1,0:T(8,128)(2,1)} %src.1), custom_call_target="tpu_custom_call" | custom-call | tf_op jit(solution)/shard_map/pallas_call | solution.py:63
  7.4 23.2 %first_exchange.1 = (bf16[4,128,1024]{2,1,0:T(8,128)(2,1)}, bf16[224,1536]{1,0:T(8,128)(2,1)}, bf16[4,56,256]{2,1,0:T(8,128)(2,1)}) custom-call(bf16[4,128,1024]{2,1,0:T(8,128)(2,1)} %shard_map.77.out_ref, bf16[56,6144]{1,0:T(8,128)(2,1)} %bitcast.13, bf16[56,1024]{1,0:T(8,128)(2,1)} %bitcast.15), custom_call_target="tpu_custom_call" | custom-call | tf_op jit(solution)/shard_map/first_exchange/pallas_call | solution.py:158
  30.6 3.5 %shard_map.78.kv_ref = bf16[3,128,1024]{2,1,0:T(8,128)(2,1)} custom-call(s32[3]{0:T(128)} %select_reduce_fusion.index, bf16[4,128,1024]{2,1,0:T(8,128)(2,1)} %get-tuple-element.11.src), custom_call_target="tpu_custom_call" | custom-call | tf_op jit(solution)/shard_map/pallas_call | solution.py:63
  34.1 37.7 %gather_head.1 = (bf16[4,4,2,3,128,256]{5,4,3,2,1,0:T(8,128)(2,1)}, bf16[4,4,2,56,256]{4,3,2,1,0:T(8,128)(2,1)}) custom-call(bf16[3,128,1024]{2,1,0:T(8,128)(2,1)} %shard_map.78.kv_ref, bf16[4,56,256]{2,1,0:T(8,128)(2,1)} %get-tuple-element.12.fz_ref), custom_call_target="tpu_custom_call" | custom-call | tf_op jit(solution)/shard_map/gather_head/pallas_call | solution.py:282
  71.8 0.0 copy-done.4
  71.9 0.0 copy-start
  71.9 1.2 copy-done
  73.0 0.0 copy-start.3
  73.0 1.1 copy-done.3
  74.1 78.8 %attend.1 = (bf16[224,1536]{1,0:T(8,128)(2,1)S(1)}, bf16[4,96,1024]{2,1,0:T(8,128)(2,1)S(1)}) custom-call(s32[14]{0:T(128)S(1)} %bitcast.10, s32[1]{0:T(128)} %bitcast.1.group, bf16[32,3,128,256]{3,2,1,0:T(8,128)(2,1)} %bitcast.11, bf16[1792,256]{1,0:T(8,128)(2,1)S(1)} %bitcast.9, bf16[224,1536]{1,0:T(8,128)(2,1)S(1)} %copy-done.3), custom_call_target="tpu_custom_call" | custom-call | tf_op jit(solution)/shard_map/attend/pallas_call | solution.py:422
  152.9 0.0 copy-start.1
  153.0 0.9 copy-done.1
  153.8 0.0 copy-start.2
  153.8 0.8 copy-done.2
  154.7 44.7 %last_exchange.1 = (bf16[56,6144]{1,0:T(8,128)(2,1)}, bf16[4,96,1024]{2,1,0:T(8,128)(2,1)}) custom-call(bf16[224,1536]{1,0:T(8,128)(2,1)} %copy-done.2, bf16[4,96,1024]{2,1,0:T(8,128)(2,1)} %copy-done.1), custom_call_target="tpu_custom_call" | custom-call | tf_op jit(solution)/shard_map/last_exchange/pallas_call | solution.py:526
  199.4 2.0 copy.10
  201.4 2.1 %copy.11 = bf16[1,1,4,96,1024]{4,3,2,1,0:T(8,128)(2,1)} copy(bf16[1,1,4,96,1024]{4,3,2,1,0:T(8,128)(2,1)} %bitcast.12) | data formatting | bytes 1572864
Async XLA Ops:
  0.6 71.2 %copy-start.4 = (s32[1,14]{1,0:T(1,128)S(1)}, s32[1,14]{1,0:T(1,128)}, u32[]{:S(2)}) copy-start(s32[1,14]{1,0:T(1,128)} %param.9) | copy-start | bytes 172
  71.9 1.2 copy-start
  73.0 1.1 copy-start.3
  152.9 0.9 copy-start.1
  153.8 0.8 copy-start.2

commit v2 on v1

--- a/solution.py
+++ b/solution.py
@@ -27,6 +27,9 @@
 STEPS = BLOCKS // CHUNK
 KEYS = CHUNK * BLOCK
 TILE = 16 * GROUP
+PAIRS = PICKED // 2
+ITEM = 2 * TILE
+STRIP = 32
 LOW = -1e30
 
 
@@ -303,36 +306,54 @@
     )(cached, fz)
 
 
-def attend_kernel(chosen, group, kv_ref, fr_ref, qx_ref, att_ref, dec_ref, kv, fresh, q, top, acc, rows32, sems):
+def attend_kernel(
+    chosen, group, kv_ref, fr_ref, qx_ref, att_ref, dec_ref,
+    kv, fresh, q, top, acc, s_a, s_b, w_a, w_b, f_a, f_b, rows32, sems,
+):
     g = group[0]
     bf16, f32 = jnp.bfloat16, jnp.float32
 
     def load(step):
         j, part = step // 4, step % 4
-        return pltpu.make_async_copy(
-            kv_ref.at[pl.ds(part * CHUNK, CHUNK), j], kv.at[pl.ds(step * CHUNK, CHUNK)], sems.at[step]
-        )
-
-    fresh_in = pltpu.make_async_copy(fr_ref, fresh, sems.at[STEPS])
-    fresh_in.start()
+        for side in range(2):
+            yield pltpu.make_async_copy(
+                kv_ref.at[pl.ds(part * CHUNK, CHUNK), j, :, pl.ds(side * DIM, DIM)],
+                kv.at[side, pl.ds(step * CHUNK, CHUNK)],
+                sems.at[side, step],
+            )
+
+    fresh_in = [
+        pltpu.make_async_copy(fr_ref.at[:, pl.ds(side * DIM, DIM)], fresh.at[side], sems.at[side, STEPS])
+        for side in range(2)
+    ]
+    for copy in fresh_in:
+        copy.start()
     for step in range(STEPS):
-        load(step).start()
+        for copy in load(step):
+            copy.start()
 
     scale = math.log2(math.e) / math.sqrt(DIM)
 
     def prepare(i, carry):
         r0 = pl.multiple_of(i * 16, 16)
+        half = (i % 2) * TILE
         for hd in range(GROUP):
-            full = qx_ref[pl.ds(r0, 16), hd * DIM : (hd + 1) * DIM].astype(f32) * scale
-            q[i, hd * 16 : (hd + 1) * 16, 0:DIM] = full.astype(bf16)
-            high = q[i, hd * 16 : (hd + 1) * 16, 0:DIM].astype(f32)
-            q[i, hd * 16 : (hd + 1) * 16, DIM:PAIR] = (full - high).astype(bf16)
-        top[i] = jnp.full((TILE, DIM), LOW, f32)
-        acc[i] = jnp.zeros((TILE, PAIR), f32)
+            to = pl.multiple_of(half + hd * 16, 16)
+            q[i // 2, pl.ds(to, 16), :] = qx_ref[pl.ds(r0, 16), hd * DIM : (hd + 1) * DIM]
         return carry
 
     lax.fori_loop(0, PICKED, prepare, 0)
-    fresh_in.wait()
+
+    def clear(p, carry):
+        top[p] = jnp.full((ITEM, DIM), LOW, f32)
+        acc[p] = jnp.zeros((ITEM, PAIR), f32)
+        return carry
+
+    lax.fori_loop(0, PAIRS, clear, 0)
+    w_b[...] = jnp.zeros((CHUNK, ITEM, DIM), bf16)
+    f_b[...] = jnp.ones((ITEM, DIM), f32)
+    for copy in fresh_in:
+        copy.wait()
 
     def before(block):
         total = jnp.int32(0)
@@ -340,40 +361,20 @@
             total = total + jnp.where(chosen[i] < block, 1, 0).astype(jnp.int32)
         return total
 
-    ones = jnp.ones((KEYS, DIM), bf16)
-
-    def fold(i, n, keys, values, mask_from):
-        qq = q[pl.ds(i, n)].reshape(n * TILE, PAIR)
-        s = lax.dot_general(qq, keys, (((1,), (1,)), ((), ())), preferred_element_type=f32)
-        if mask_from is not None:
-            row = lax.broadcasted_iota(jnp.int32, (TILE, KEYS), 0)
-            token = 64 * ((row % 16) // 8) + 8 * g + row % 8
-            key = lax.broadcasted_iota(jnp.int32, (TILE, KEYS), 1)
-            s = jnp.where(key <= token + mask_from, s, LOW)
-        old = top[pl.ds(i, n)].reshape(n * TILE, DIM)
-        new = jnp.maximum(old, jnp.max(s, axis=1, keepdims=True))
-        w = jnp.exp2(s - new[:, 0:1]).astype(bf16)
-        part = jnp.dot(w, values, preferred_element_type=f32)
-        factor = jnp.exp2(old - new)
-        both = jnp.concatenate([factor, factor], axis=1)
-        acc[pl.ds(i, n)] = (acc[pl.ds(i, n)].reshape(n * TILE, PAIR) * both + part).reshape(n, TILE, PAIR)
-        top[pl.ds(i, n)] = new.reshape(n, TILE, DIM)
-
-    def step_body(step, first):
-        load(step).wait()
-        last = before((step + 1) * CHUNK)
+    def make_ready(step):
+        for copy in load(step):
+            copy.wait()
 
         def patch(i, carry):
-            kv[chosen[i]] = fresh[pl.ds(pl.multiple_of(i * BLOCK, BLOCK), BLOCK), :]
+            for side in range(2):
+                kv[side, chosen[i]] = fresh[side, pl.ds(pl.multiple_of(i * BLOCK, BLOCK), BLOCK), :]
             return carry
 
-        lax.fori_loop(first, last, patch, 0)
-
+        lax.fori_loop(before(step * CHUNK), before((step + 1) * CHUNK), patch, 0)
         at = step * CHUNK
-        slab = kv[pl.ds(at, CHUNK), pl.ds(pl.multiple_of(g * 16, 16), 16), :].astype(f32)
-        flat = slab.reshape(CHUNK * 16, PAIR)
         for side in range(2):
-            rows32[side] = flat[:, side * DIM : (side + 1) * DIM]
+            slab = kv[side, pl.ds(at, CHUNK), pl.ds(pl.multiple_of(g * 16, 16), 16), :].astype(f32)
+            rows32[side] = slab.reshape(CHUNK * 16, DIM)
         for k in range(4):
             for u in range(4):
                 for side in range(2):
@@ -381,36 +382,108 @@
                     to = u * PAIR + side * DIM
                     dec_ref[k, pl.ds(pl.multiple_of(at, CHUNK), CHUNK), to : to + DIM] = line.astype(bf16)
 
-        both = kv[pl.ds(at, CHUNK)].reshape(KEYS, PAIR)
-        keys = jnp.concatenate([both[:, :DIM], both[:, :DIM]], axis=1)
-        values = jnp.concatenate([both[:, DIM:], ones], axis=1)
-
-        def diagonal(i, carry):
-            fold(i, 1, keys, values, (chosen[i] - at) * BLOCK)
-            return carry
-
-        lax.fori_loop(first, last, diagonal, 0)
-        left = PICKED - last
-        odd = left % 2
-
-        @pl.when(odd == 1)
-        def _():
-            fold(last, 1, keys, values, None)
-
-        def two(t, carry):
-            fold(last + odd + 2 * t, 2, keys, values, None)
-            return carry
-
-        lax.fori_loop(0, left // 2, two, 0)
-        return last
-
-    lax.fori_loop(0, STEPS, step_body, jnp.int32(0))
+    ones = jnp.ones((KEYS, DIM), bf16)
+
+    def scores(p, step, s):
+        keys = kv[0, pl.ds(step * CHUNK, CHUNK)].reshape(KEYS, DIM)
+        s[...] = lax.dot_general(q[p], keys, (((1,), (1,)), ((), ())), preferred_element_type=f32)
+
+    def hide(p, step, s, dead):
+        for side in range(2):
+            rows = slice(side * TILE, (side + 1) * TILE)
+            own = jnp.where(dead, -1, chosen[2 * p + side] - step * CHUNK)
+
+            def blank(j, carry):
+                s[rows, pl.ds(pl.multiple_of(j * BLOCK, BLOCK), BLOCK)] = jnp.full((TILE, BLOCK), LOW, f32)
+                return carry
+
+            lax.fori_loop(jnp.clip(own + 1, 0, CHUNK), CHUNK, blank, 0)
+
+            @pl.when(jnp.logical_and(own >= 0, own < CHUNK))
+            def _():
+                cols = pl.ds(pl.multiple_of(own * BLOCK, BLOCK), BLOCK)
+                row = lax.broadcasted_iota(jnp.int32, (TILE, BLOCK), 0)
+                token = 64 * ((row % 16) // 8) + 8 * g + row % 8
+                key = lax.broadcasted_iota(jnp.int32, (TILE, BLOCK), 1)
+                s[rows, cols] = jnp.where(key <= token, s[rows, cols], LOW)
+
+    def soften(p, s, w, f, lo, hi):
+        for r in range(lo, hi, STRIP):
+            rows = slice(r, r + STRIP)
+            parts = [s[rows, j * DIM : (j + 1) * DIM] for j in range(CHUNK)]
+            best = functools.reduce(jnp.maximum, parts)
+            old = top[p, rows, :]
+            new = jnp.maximum(old, jnp.max(best, axis=1, keepdims=True))
+            for j in range(CHUNK):
+                w[j, rows, :] = jnp.exp2((parts[j] - new) * scale).astype(bf16)
+            f[rows, :] = jnp.exp2((old - new) * scale)
+            top[p, rows, :] = new
+
+    def mix(p, step, w, f, lo, hi):
+        values = jnp.concatenate([kv[1, pl.ds(step * CHUNK, CHUNK)].reshape(KEYS, DIM), ones], axis=1)
+        weights = jnp.concatenate([w[j, lo:hi, :] for j in range(CHUNK)], axis=1)
+        part = jnp.dot(weights, values, preferred_element_type=f32)
+        factor = f[lo:hi, :]
+        acc[p, lo:hi, :] = acc[p, lo:hi, :] * jnp.concatenate([factor, factor], axis=1) + part
+
+    def last_of(p):
+        return chosen[2 * p + 1] // CHUNK
+
+    total = jnp.int32(0)
+    for p in range(PAIRS):
+        total = total + last_of(p) + 1
+
+    def following(item):
+        p, step = item
+        more = step < last_of(p)
+        return (
+            jnp.where(more, p, jnp.minimum(p + 1, PAIRS - 1)),
+            jnp.where(more, step + 1, 0),
+        )
+
+    def turn(t, ready, last, now, s_now, s_next, w_now, w_last, f_now, f_last):
+        after = following(now)
+        fits = after[1] < ready
+
+        @pl.when(jnp.logical_not(fits))
+        def _():
+            make_ready(after[1])
+
+        dead = t >= total
+        @pl.when(jnp.logical_or(dead, chosen[2 * now[0]] < (now[1] + 1) * CHUNK))
+        def _():
+            hide(now[0], now[1], s_now, dead)
+
+        scores(after[0], after[1], s_next)
+        for lo in range(0, ITEM, TILE):
+            soften(now[0], s_now, w_now, f_now, lo, lo + TILE)
+            mix(now[0], now[1], w_now, f_now, lo, lo + TILE)
+        return jnp.where(fits, ready, after[1] + 1), now, after
+
+    def both_turns(i, carry):
+        ready, last, now = carry
+        ready, last, now = turn(2 * i, ready, last, now, s_a, s_b, w_a, w_b, f_a, f_b)
+        ready, last, now = turn(2 * i + 1, ready, last, now, s_b, s_a, w_b, w_a, f_b, f_a)
+        return ready, last, now
+
+    make_ready(0)
+    zero = jnp.int32(0)
+    scores(0, 0, s_a)
+    ready, last, now = lax.fori_loop(0, (total + 1) // 2, both_turns, (jnp.int32(1), (zero, zero), (zero, zero)))
+
+    def rest(step, carry):
+        make_ready(step)
+        return carry
+
+    lax.fori_loop(ready, STEPS, rest, 0)
 
     def finish(i, carry):
-        out = acc[i, :, 0:DIM] / acc[i, :, DIM:PAIR]
+        half = (i % 2) * TILE
         r0 = pl.multiple_of(i * 16, 16)
         for hd in range(GROUP):
-            att_ref[pl.ds(r0, 16), hd * DIM : (hd + 1) * DIM] = out[hd * 16 : (hd + 1) * 16].astype(bf16)
+            rows = pl.ds(pl.multiple_of(half + hd * 16, 16), 16)
+            out = acc[i // 2, rows, 0:DIM] / acc[i // 2, rows, DIM:PAIR]
+            att_ref[pl.ds(r0, 16), hd * DIM : (hd + 1) * DIM] = out.astype(bf16)
         return carry
 
     lax.fori_loop(0, PICKED, finish, 0)
@@ -428,44 +501,50 @@
         in_specs=[smem, smem, ANY, ANY, IN_VMEM],
         out_specs=(IN_VMEM, IN_VMEM),
         scratch_shapes=[
-            pltpu.VMEM((BLOCKS, BLOCK, PAIR), bf16),
-            pltpu.VMEM((PICKED * BLOCK, PAIR), bf16),
-            pltpu.VMEM((PICKED, TILE, PAIR), bf16),
-            pltpu.VMEM((PICKED, TILE, DIM), f32),
-            pltpu.VMEM((PICKED, TILE, PAIR), f32),
+            pltpu.VMEM((2, BLOCKS, BLOCK, DIM), bf16),
+            pltpu.VMEM((2, PICKED * BLOCK, DIM), bf16),
+            pltpu.VMEM((PAIRS, ITEM, DIM), bf16),
+            pltpu.VMEM((PAIRS, ITEM, DIM), f32),
+            pltpu.VMEM((PAIRS, ITEM, PAIR), f32),
+            pltpu.VMEM((ITEM, KEYS), f32),
+            pltpu.VMEM((ITEM, KEYS), f32),
+            pltpu.VMEM((CHUNK, ITEM, DIM), bf16),
+            pltpu.VMEM((CHUNK, ITEM, DIM), bf16),
+            pltpu.VMEM((ITEM, DIM), f32),
+            pltpu.VMEM((ITEM, DIM), f32),
             pltpu.VMEM((2, CHUNK * 16, DIM), f32),
-            pltpu.SemaphoreType.DMA((STEPS + 1,)),
+            pltpu.SemaphoreType.DMA((2, STEPS + 1)),
         ],
-        compiler_params=pltpu.CompilerParams(vmem_limit_bytes=48 * 1024 * 1024),
+        compiler_params=pltpu.CompilerParams(vmem_limit_bytes=58 * 1024 * 1024),
         name="attend",
     )(chosen, group, kv, fresh, qx)
 
 
-def last_kernel(att_ref, dec_ref, out_ref, laid_ref, a_send, a_recv, d_send, d_recv):
+def last_kernel(
+    att_ref, dec_ref, out_ref, laid_ref, mid, a_send, a_recv, z_send, z_recv, y_send, y_recv
+):
     y, s, x, z, c = here()
     g = 2 * x + c
     barrier = pltpu.get_barrier_semaphore()
     greet_plane(barrier, y, s)
-    giver = s // 4
     for d in range(1, POOL):
-        source = seat(giver // 2, y, giver % 2)
-        pl.semaphore_signal(barrier, inc=1, device_id=((y + d) % POOL, source), device_id_type=MESH)
-    pl.semaphore_wait(barrier, 31 + jnp.where(z == y, 0, 4))
+        pl.semaphore_signal(barrier, inc=1, device_id=((y + d) % POOL, s), device_id_type=MESH)
+    pl.semaphore_wait(barrier, 31 + POOL - 1)
 
     def slab(k):
-        return dec_ref.at[k], laid_ref.at[y], 4 * g + k
+        to_z, to_c = 2 * c + k // 2, k % 2
+        return dec_ref.at[k], mid.at[z], seat(x, to_z, to_c)
 
     def slab_send(k, carry):
         src, dst, to = slab(k)
-        mine = jnp.logical_and(z == y, to == s)
-
-        @pl.when(jnp.logical_not(mine))
-        def _():
-            remote(src, dst, d_send.at[k], d_recv, z, to).start()
-
-        @pl.when(mine)
-        def _():
-            pltpu.make_async_copy(src, dst, d_recv).start()
+
+        @pl.when(to != s)
+        def _():
+            remote(src, dst, z_send.at[k], z_recv.at[z], y, to).start()
+
+        @pl.when(to == s)
+        def _():
+            pltpu.make_async_copy(src, dst, z_recv.at[z]).start()
 
         return carry
 
@@ -494,13 +573,29 @@
 
     lax.fori_loop(0, 28, send, 0)
 
+    passing = []
+    for d in (0, 1, 3, 2):
+        h = (z + d) % 4
+        remote(mid.at[h], mid.at[h], y_send.at[d], z_recv.at[h], y, (s + 1) % 32).wait_recv()
+        copy = remote(mid.at[h], laid_ref.at[y], y_send.at[d], y_recv, h, s)
+        own = pltpu.make_async_copy(mid.at[h], laid_ref.at[y], y_recv)
+
+        @pl.when(h != y)
+        def _():
+            copy.start()
+
+        @pl.when(h == y)
+        def _():
+            own.start()
+
+        passing.append((h, copy))
+
     def slab_sent(k, carry):
         src, dst, to = slab(k)
-        mine = jnp.logical_and(z == y, to == s)
-
-        @pl.when(jnp.logical_not(mine))
-        def _():
-            remote(src, dst, d_send.at[k], d_recv, z, to).wait_send()
+
+        @pl.when(to != s)
+        def _():
+            remote(src, dst, z_send.at[k], z_recv.at[z], y, to).wait_send()
 
         return carry
 
@@ -516,8 +611,14 @@
         return carry
 
     lax.fori_loop(0, 28, sent, 0)
+    for h, copy in passing:
+
+        @pl.when(h != y)
+        def _():
+            copy.wait_send()
+
     remote(out_ref, out_ref, a_send.at[0], a_recv, y, (s + 1) % 32).wait_recv()
-    remote(laid_ref, laid_ref, d_send.at[0], d_recv, y, (s + 1) % 32).wait_recv()
+    remote(laid_ref, laid_ref, y_send.at[0], y_recv, y, (s + 1) % 32).wait_recv()
 
 
 def last_exchange(att, dec):
@@ -529,10 +630,14 @@
             jax.ShapeDtypeStruct((ROWS, HEADS * WIDE), bf16),
             jax.ShapeDtypeStruct((POOL, BLOCKS, 1024), bf16),
         ),
-        in_specs=[ANY, ANY],
-        out_specs=(ANY, ANY),
-        scratch_shapes=[dma((28,)), dma, dma((4,)), dma],
-        compiler_params=pltpu.CompilerParams(collective_id=2, has_side_effects=True),
+        in_specs=[IN_VMEM, IN_VMEM],
+        out_specs=(IN_VMEM, IN_VMEM),
+        scratch_shapes=[
+            pltpu.VMEM((4, BLOCKS, 1024), bf16), dma((28,)), dma, dma((4,)), dma((4,)), dma((4,)), dma,
+        ],
+        compiler_params=pltpu.CompilerParams(
+            collective_id=2, has_side_effects=True, vmem_limit_bytes=16 * 1024 * 1024
+        ),
         name="last_exchange",
     )(att, dec)
 

time: 203 us -> 142 us (0.70)
  Pallas kernels: 192 us -> 136 us
  local copies, waits for them, and re-layouts: 8.13 us -> 4.04 us
    pallas_call x1, Pallas kernels: 78.8 us -> 42 us  [attend(): pl.pallas_call(attend_kernel, out_shape=(jax.ShapeDtypeStruct((4 * ROWS,...]
    pallas_call x1, Pallas kernels: 44.7 us -> 25.1 us  [last_exchange(): pl.pallas_call(last_kernel, out_shape=(jax.ShapeDtypeStruct((ROWS, HEADS...]
    unnamed x12 -> x6, local copies, waits for them, and re-layouts: 8.05 us -> 3.96 us
where the time goes in v2:
time: 142 us; the launch traced here: 143 us
  Pallas kernels  136 us (96%)
  local copies, waits for them, and re-layouts  4.04 us (3%)
  other arithmetic  2.65 us (2%)
    pallas_call x1, Pallas kernels, attend(): pl.pallas_call(attend_kernel, out_shape=(jax.ShapeDtypeStruct((4 * ROWS,...  42 us
    pallas_call x1, Pallas kernels, gather_head(): pl.pallas_call(gather_kernel, out_shape=(jax.ShapeDtypeStruct((4, 4, 2, S...  37.7 us
    pallas_call x1, Pallas kernels, last_exchange(): pl.pallas_call(last_kernel, out_shape=(jax.ShapeDtypeStruct((ROWS, HEADS...  25.1 us
    pallas_call x1, Pallas kernels, first_exchange(): pl.pallas_call(first_kernel, out_shape=(jax.ShapeDtypeStruct((POOL, BLOCK...  23.2 us
    pallas_call x2, Pallas kernels, pick_blocks(): pl.pallas_call(pick_kernel, out_shape=jax.ShapeDtypeStruct((count, rows,...  7.56 us
    unnamed x6, local copies, waits for them, and re-layouts  3.96 us

profile of v2, /device:TPU:1, one launch (start us, length us, event | category | flops | bytes accessed | tf_op | source)
XLA Modules:
  0.0 142.9 jit_solution(3210643088130936698)
XLA Ops:
  0.7 0.7 compare_select_fusion
  1.3 1.3 select_reduce_fusion.index
  2.7 0.1 reshape.19
  2.8 0.6 reduce_sum.19.index
  3.4 4.0 %shard_map.77.out_ref = bf16[4,128,1024]{2,1,0:T(8,128)(2,1)} custom-call(s32[4]{0:T(128)} %reduce_sum.19.index, bf16[4,128,1024]{2,1,0:T(8,128)(2,1)} %src.1), custom_call_target="tpu_custom_call" | custom-call | tf_op jit(solution)/shard_map/pallas_call | solution.py:66
  7.4 23.2 %first_exchange.1 = (bf16[4,128,1024]{2,1,0:T(8,128)(2,1)}, bf16[224,1536]{1,0:T(8,128)(2,1)}, bf16[4,56,256]{2,1,0:T(8,128)(2,1)}) custom-call(bf16[4,128,1024]{2,1,0:T(8,128)(2,1)} %shard_map.77.out_ref, bf16[56,6144]{1,0:T(8,128)(2,1)} %bitcast.13, bf16[56,1024]{1,0:T(8,128)(2,1)} %bitcast.14), custom_call_target="tpu_custom_call" | custom-call | tf_op jit(solution)/shard_map/first_exchange/pallas_call | solution.py:161
  30.6 3.5 %shard_map.78.kv_ref = bf16[3,128,1024]{2,1,0:T(8,128)(2,1)} custom-call(s32[3]{0:T(128)} %select_reduce_fusion.index, bf16[4,128,1024]{2,1,0:T(8,128)(2,1)} %get-tuple-element.11.src), custom_call_target="tpu_custom_call" | custom-call | tf_op jit(solution)/shard_map/pallas_call | solution.py:66
  34.1 37.7 %gather_head.1 = (bf16[4,4,2,3,128,256]{5,4,3,2,1,0:T(8,128)(2,1)}, bf16[4,4,2,56,256]{4,3,2,1,0:T(8,128)(2,1)}) custom-call(bf16[3,128,1024]{2,1,0:T(8,128)(2,1)} %shard_map.78.kv_ref, bf16[4,56,256]{2,1,0:T(8,128)(2,1)} %get-tuple-element.12.fz_ref), custom_call_target="tpu_custom_call" | custom-call | tf_op jit(solution)/shard_map/gather_head/pallas_call | solution.py:285
  71.8 42.0 %attend.1 = (bf16[224,1536]{1,0:T(8,128)(2,1)}, bf16[4,96,1024]{2,1,0:T(8,128)(2,1)}) custom-call(s32[14]{0:T(128)} %bitcast.15, s32[1]{0:T(128)} %bitcast.1.group, bf16[32,3,128,256]{3,2,1,0:T(8,128)(2,1)} %bitcast.11, bf16[1792,256]{1,0:T(8,128)(2,1)} %bitcast.12, bf16[224,1536]{1,0:T(8,128)(2,1)} %get-tuple-element.15.qx_ref), custom_call_target="tpu_custom_call" | custom-call | tf_op jit(solution)/shard_map/attend/pallas_call | solution.py:495
  113.8 0.0 copy-start
  113.8 1.1 copy-done
  115.0 0.0 copy-start.1
  115.0 1.1 copy-done.1
  116.1 25.1 %last_exchange.1 = (bf16[56,6144]{1,0:T(8,128)(2,1)S(1)}, bf16[4,96,1024]{2,1,0:T(8,128)(2,1)S(1)}) custom-call(bf16[224,1536]{1,0:T(8,128)(2,1)S(1)} %copy-done.1, bf16[4,96,1024]{2,1,0:T(8,128)(2,1)S(1)} %copy-done), custom_call_target="tpu_custom_call" | custom-call | tf_op jit(solution)/shard_map/last_exchange/pallas_call | solution.py:627
  141.2 0.8 copy.10
  142.1 0.9 copy.11
Async XLA Ops:
  113.8 1.1 copy-start
  115.0 1.1 copy-start.1
